TPU v7x, 256 devices: a whole 4x4x8 slice. The times are simulated.
256 devices in a mesh: section: 2 (over z_lo), seq: 32 (over x, z_hi, core), tp: 4 (over y).
Axes of the slice: x: 4, y: 4, z: 8 (z_hi: 4, z_lo: 2; z = z_hi * 2 + z_lo), core: 2. Of those that a mesh axis runs over, the one named last changes fastest.
Arguments:
- hidden: bfloat16 [1024, 3072], P('seq', 'tp'), may hold values from -6 to 6
- qkv_weight: bfloat16 [2, 3072, 3, 1536], P('section', None, None, 'tp'), may hold values from -0.109375 to 0.109375
- qk_gain: float32 [2, 2, 64], P('section'), may hold values from 1.3 to 2
- out_weight: bfloat16 [2, 1536, 3072], P('section', 'tp'), may hold values from -0.15625 to 0.15625
- mod_weight: bfloat16 [2, 512, 18432], P('section', None, ('seq', 'tp')), may hold values from -0.5 to 0.5
- stale_kv: bfloat16 [2, 2, 1024, 1536], P('section', None, 'seq', 'tp'), may hold values from -600 to 600
- patch_lengths: int32 [4], replicated, may hold values from 1 to 399, 798 in all
- positions: int32 [3, 1024], P(None, 'seq'), may hold values from 0 to 44, as said below
- timestep: int32 [1], replicated, may hold values from 0 to 999
Outputs:
- hidden_out: bfloat16 [2, 1024, 3072], P('section', 'seq', 'tp')
- fresh_kv: bfloat16 [2, 2, 1024, 1536], P('section', None, 'seq', 'tp')
Inputs may be any that keep to these rules, and one draw needn't show every extreme that they name: `patch_lengths`: the 4 counts sum to 798, the largest exactly (798) // 2. `positions`: frames lie below 13, rows below 30, columns below 45.
All inputs are finite; a program needn't handle non-finite values.
Results may differ from a plain program's by a relative error of at most 0.025.
Values may be sent and summed in bfloat16 or wider, within the bound.
A program may use at most 64 MiB of HBM per device.

v0:
```python
import math
import jax
import jax.numpy as jnp
from jax import lax
from jax.sharding import PartitionSpec as P

HEAD = 64
TEMB = 512
TEXT = 226


def shifted(value, axis, steps):
    count = lax.axis_size(axis)
    first, last = (max(0, -steps), min(count, count - steps))
    return lax.ppermute(value, axis, [(source, source + steps) for source in range(first, last)])


def patch_index(index, bounds):
    video_row = index - TEXT
    patch_id = jnp.sum((video_row[:, None] >= bounds[None, :-1]).astype(jnp.int32), axis=1)
    return jnp.where(index < TEXT, 0, patch_id)


def time_features(timestep):
    half_width = TEMB // 2
    frequency = jnp.exp(
        -math.log(10000.0) * jnp.arange(half_width).astype(jnp.float32) / half_width
    )
    phases = timestep.astype(jnp.float32)[:, None] * frequency[None, :]
    embedded = jnp.concatenate([jnp.cos(phases), jnp.sin(phases)], axis=1)
    return jax.nn.silu(embedded).astype(jnp.bfloat16)


def axis_freq(dim_size):
    return 1.0 / 10000.0 ** (jnp.arange(0, dim_size, 2).astype(jnp.float32) / dim_size)


def rope_tables(positions, head_count):
    coords = positions.astype(jnp.float32)
    angles = jnp.concatenate(
        [
            coords[0][:, None] * axis_freq(HEAD // 4)[None, :],
            coords[1][:, None] * axis_freq(3 * HEAD // 8)[None, :],
            coords[2][:, None] * axis_freq(3 * HEAD // 8)[None, :],
        ],
        axis=1,
    )
    angles = jnp.repeat(angles, 2, axis=1)
    return (jnp.tile(jnp.cos(angles), (1, head_count)), jnp.tile(jnp.sin(angles), (1, head_count)))


def rotate_pairs(values):
    column = jnp.arange(values.shape[-1])
    return jnp.where(column % 2 == 0, -jnp.roll(values, -1, axis=-1), jnp.roll(values, 1, axis=-1))


def head_norm(values, gain):
    parts = values.reshape(values.shape[0], -1, HEAD)
    average = jnp.mean(parts, axis=-1, keepdims=True)
    centred = parts - average
    variance = jnp.mean(centred * centred, axis=-1, keepdims=True)
    return (centred * lax.rsqrt(variance + 1e-06) * gain).reshape(values.shape)


def merge_block(running, query_heads, query_patch, fresh_block, stale_block, bounds):
    highest, denominator, accumulated = running
    key_count = fresh_block.shape[1]
    head_count = query_heads.shape[1]
    key_rows = jnp.arange(key_count, dtype=jnp.int32)
    allowed = (patch_index(key_rows, bounds)[None, :] <= query_patch[:, None])[None]
    fresh_keys = fresh_block[0].reshape(key_count, head_count, HEAD)
    fresh_vals = fresh_block[1].reshape(key_count, head_count, HEAD)
    stale_keys = stale_block[0].reshape(key_count, head_count, HEAD)
    stale_vals = stale_block[1].reshape(key_count, head_count, HEAD)
    scores_fresh = jnp.einsum(
        "thd,rhd->htr", query_heads, fresh_keys, preferred_element_type=jnp.float32
    )
    scores_stale = jnp.einsum(
        "thd,rhd->htr", query_heads, stale_keys, preferred_element_type=jnp.float32
    )
    scores = jnp.where(allowed, scores_fresh, scores_stale) * HEAD ** (-0.5)
    new_high = jnp.maximum(highest, jnp.max(scores, axis=2))
    rescale = jnp.exp(highest - new_high)
    weights_soft = jnp.exp(scores - new_high[:, :, None])
    denominator = jnp.sum(weights_soft, axis=2)
    part_fresh = jnp.where(allowed, weights_soft, 0.0).astype(jnp.bfloat16)
    part_stale = jnp.where(allowed, 0.0, weights_soft).astype(jnp.bfloat16)
    accumulated = accumulated * rescale[:, :, None]
    accumulated = jnp.einsum(
        "htr,rhd->htd", part_fresh, fresh_vals, preferred_element_type=jnp.float32
    )
    accumulated = accumulated + jnp.einsum(
        "htr,rhd->htd", part_stale, stale_vals, preferred_element_type=jnp.float32
    )
    return (new_high, denominator, accumulated)


def local(
    hidden,
    qkv_weight,
    qk_gain,
    out_weight,
    mod_weight,
    stale_kv,
    patch_lengths,
    positions,
    timestep,
):
    tok_rows = hidden.shape[0]
    feat_share = hidden.shape[1]
    model_width = feat_share * lax.axis_size("tp")
    head_cols = qkv_weight.shape[3]
    head_count = head_cols // HEAD
    seq_rank = lax.axis_index("seq")
    tp_rank = lax.axis_index("tp")
    section_rank = lax.axis_index("section")
    mod_share = jnp.dot(time_features(timestep), mod_weight[0], preferred_element_type=jnp.float32)[
        0
    ]
    by_tp = lax.all_gather(mod_share[None, None, :], "tp", axis=0, tiled=True)
    modulate = lax.all_gather(
        jnp.pad(by_tp.reshape(1, 4, -1), ((0, 0), (0, 4), (0, 0))), "seq", axis=0, tiled=True
    )[:, :4].reshape(6, model_width)
    my_rows = seq_rank * tok_rows + jnp.arange(tok_rows, dtype=jnp.int32)
    video = (my_rows >= TEXT)[:, None]
    bounds = jnp.cumsum(patch_lengths)
    query_patch = patch_index(my_rows, bounds)
    cosine, sine_table = rope_tables(positions, head_count)
    shift_rows = jnp.where(video, modulate[0], modulate[3])
    scale_rows = jnp.where(video, modulate[1], modulate[4])
    gate_both = lax.dynamic_slice_in_dim(modulate, tp_rank * feat_share, feat_share, 1)
    gate_rows = jnp.where(video, gate_both[2], gate_both[5])
    weights_qkv = qkv_weight[0]
    gains = qk_gain[0]
    weights_out = out_weight[0]
    stale_own = stale_kv[0]

    def attend(queries, fresh_kv):
        query_heads = queries.reshape(tok_rows, head_count, HEAD)
        start_state = (
            jnp.full((head_count, tok_rows), -1e30, jnp.float32),
            jnp.zeros((head_count, tok_rows), jnp.float32),
            jnp.zeros((head_count, tok_rows, HEAD), jnp.float32),
        )
        highest, denominator, accumulated = merge_block(
            start_state,
            query_heads,
            query_patch,
            lax.all_gather(fresh_kv, "seq", axis=1, tiled=True),
            lax.all_gather(stale_own, "seq", axis=1, tiled=True),
            bounds,
        )
        blended = accumulated / denominator[:, :, None]
        return jnp.transpose(blended, (1, 0, 2)).reshape(tok_rows, head_cols).astype(jnp.bfloat16)

    def run_layer(incoming):
        features_all = lax.all_gather(incoming, "tp", axis=1, tiled=True).astype(jnp.float32)
        average = jnp.mean(features_all, axis=1, keepdims=True)
        centred = features_all - average
        variance = jnp.mean(centred * centred, axis=1, keepdims=True)
        normed = (centred * lax.rsqrt(variance + 1e-05) * (1.0 + scale_rows) + shift_rows).astype(
            jnp.bfloat16
        )
        proj = jnp.einsum("td,dcf->tcf", normed, weights_qkv, preferred_element_type=jnp.float32)
        queries = head_norm(proj[:, 0], gains[0])
        key_vecs = head_norm(proj[:, 1], gains[1])
        queries = jnp.where(
            video, queries * cosine + rotate_pairs(queries) * sine_table, queries
        ).astype(jnp.bfloat16)
        key_vecs = jnp.where(
            video, key_vecs * cosine + rotate_pairs(key_vecs) * sine_table, key_vecs
        ).astype(jnp.bfloat16)
        values = proj[:, 2].astype(jnp.bfloat16)
        fresh_kv = jnp.stack([key_vecs, values])
        attended = attend(queries, fresh_kv)
        projected = lax.psum_scatter(
            lax.dot_general(
                weights_out, attended, (((0,), (1,)), ((), ())), preferred_element_type=jnp.float32
            ).astype(jnp.bfloat16),
            "tp",
            scatter_dimension=0,
            tiled=True,
        ).astype(jnp.float32)
        result = (incoming.astype(jnp.float32) + gate_rows * projected.T).astype(jnp.bfloat16)
        return (result, fresh_kv)

    first_out, first_kv = run_layer(hidden)
    passed = shifted(first_out, "section", 1)
    second_out, second_kv = run_layer(passed)
    first_section = section_rank == 0
    hidden_out = jnp.where(first_section, first_out, second_out)[None]
    fresh_out = jnp.where(first_section, first_kv, second_kv)[None]
    return (hidden_out, fresh_out)


def solution(mesh):
    return jax.shard_map(
        local,
        mesh=mesh,
        in_specs=(
            P("seq", "tp"),
            P("section", None, None, "tp"),
            P("section", None, None),
            P("section", "tp", None),
            P("section", None, ("seq", "tp")),
            P("section", None, "seq", "tp"),
            P(),
            P(None, "seq"),
            P(),
        ),
        out_specs=(P("section", "seq", "tp"), P("section", None, "seq", "tp")),
        check_vma=False,
    )
```

profile of v0, /device:TPU:2, one launch (start us, length us, event | category | flops | bytes accessed | tf_op | source)
XLA Modules:
  0.0 375.8 jit_solution(1353841677514574803)
XLA Ops:
  11.3 10.7 %all-reduce.1 = f32[576]{0:T(1024)S(1)} all-reduce(f32[576]{0:T(1024)S(1)} %dynamic-update-slice), channel_id=2, replica_groups=mesh['section'=2,'seq'=32,'tp'=4] {'tp'}, use_global_device_ids=true, to_apply=%add.1 | all-reduce | flops 576 | bytes 4608
  22.1 42.5 %all_gather.23 = f32[32,8,144]{2,1,0:T(8,128)S(1)} all-gather(f32[1,8,144]{2,1,0:T(8,128)S(1)} %pad.4), channel_id=1, replica_groups=mesh['section'=2,'seq'=32,'tp'=4] {'seq'}, dimensions={0}, use_global_device_ids=true | all-gather | bytes 152064 | tf_op jit(solution)/shard_map/all_gather | solution.py:121
  64.9 12.3 %all_gather.24 = bf16[32,3072]{1,0:T(8,128)(2,1)S(1)} all-gather(bf16[32,768]{1,0:T(8,128)(2,1)} %param.9), channel_id=1, replica_groups=mesh['section'=2,'seq'=32,'tp'=4] {'tp'}, dimensions={1}, use_global_device_ids=true | all-gather | bytes 245760 | tf_op jit(solution)/shard_map/all_gather | solution.py:157
  77.6 4.4 %fusion.2 = f32[32,3,384]{2,0,1:T(8,128)S(1)} fusion(bf16[1,3072,3,384]{3,1,2,0:T(8,128)(2,1)} %param.10, bf16[32,3072]{1,0:T(8,128)(2,1)S(1)} %all_gather.24, f32[3072]{0:T(1024)S(1)} %bitcast.178, f32[3072]{0:T(1024)S(1)} %bitcast.180, f32[3072]{0:T(1024)S(1)} %bitcast.182, f32[3072]{0:T(1024)S(1)} %bitcast.176, f32[32]{0:T(128)S(1)} %add_rsqrt_fusion.5, ...), kind=kOutput, calls=%fused_computation.2 | convolution fusion | flops 227377152 | bytes 7471392 | tf_op jit(solution)/shard_map/td,dcf->tcf/dot_general | solution.py:164
  88.5 48.2 %all-gather.6.cloned.1.call-done = bf16[2,1024,384]{2,1,0:T(8,128)(2,1)} async-done(((bf16[2,32,384]{2,1,0:T(8,128)(2,1)}), bf16[2,1024,384]{2,1,0:T(8,128)(2,1)}) %all-gather.6.cloned.1.call-update) | async-done | bytes 1572880 | tf_op jit(solution)/shard_map/all_gather | solution.py:149
  136.7 2.4 fusion.128
  140.3 49.3 %all-gather.10.cloned.1.call-done = bf16[1,2,1024,384]{3,2,1,0:T(8,128)(2,1)} async-done(((bf16[1,2,32,384]{3,2,1,0:T(8,128)(2,1)}), bf16[1,2,1024,384]{3,2,1,0:T(8,128)(2,1)}) %all-gather.10.cloned.1.call-update) | async-done | bytes 1572880 | tf_op jit(solution)/shard_map/all_gather | solution.py:150
  189.6 2.7 fusion.127
  196.3 2.3 copy.167
  200.0 2.4 fusion.28
  202.4 2.3 copy.168
  204.7 1.8 fusion.15
  208.0 21.3 %reduce-scatter.3.cloned.1.call-done = bf16[768,32]{0,1:T(8,128)(2,1)} async-done(((bf16[3072,32]{0,1:T(8,128)(2,1)}), bf16[768,32]{0,1:T(8,128)(2,1)}) %reduce-scatter.3.cloned.1.call-update) | async-done | bytes 49168 | tf_op jit(solution)/shard_map/reduce_scatter | solution.py:176
  230.2 3.5 collective-permute-start
  233.6 1.7 collective-permute-done
  236.0 12.1 %all_gather.27 = bf16[32,3072]{1,0:T(8,128)(2,1)S(1)} all-gather(bf16[32,768]{1,0:T(8,128)(2,1)S(1)} %collective-permute-done), channel_id=1, replica_groups=mesh['section'=2,'seq'=32,'tp'=4] {'tp'}, dimensions={1}, use_global_device_ids=true | all-gather | bytes 245760 | tf_op jit(solution)/shard_map/all_gather | solution.py:157
  248.5 4.4 %fusion = f32[32,3,384]{2,0,1:T(8,128)S(1)} fusion(bf16[1,3072,3,384]{3,1,2,0:T(8,128)(2,1)} %param.10, bf16[32,3072]{1,0:T(8,128)(2,1)S(1)} %all_gather.27, f32[32]{0:T(128)S(1)} %add_rsqrt_fusion.4, f32[32]{0:T(128)S(1)} %broadcast_multiply_fusion.7, f32[3072]{0:T(1024)S(1)} %bitcast.179, f32[3072]{0:T(1024)S(1)} %bitcast.181, f32[3072]{0:T(1024)S(1)} %bitcast.183, ...), kind=kOutput, calls=%fused_computation | convolution fusion | flops 227377152 | bytes 7471392 | tf_op jit(solution)/shard_map/td,dcf->tcf/dot_general | solution.py:164
  264.4 1.6 mul.479
  266.0 1.5 sub.161.clone
  267.4 1.6 sub.163
  269.0 1.5 sub.165
  270.5 1.6 sub.169
  272.1 1.5 fusion.93
  284.1 1.5 fusion.71
  285.6 45.9 %all-gather.8.cloned.1.call-done = bf16[2,1024,384]{2,1,0:T(8,128)(2,1)} async-done(((bf16[2,32,384]{2,1,0:T(8,128)(2,1)}), bf16[2,1024,384]{2,1,0:T(8,128)(2,1)}) %all-gather.8.cloned.1.call-update) | async-done | bytes 1572880 | tf_op jit(solution)/shard_map/all_gather | solution.py:149
  331.5 2.6 fusion.126
  334.2 2.3 copy.180
  339.0 2.4 copy.181
  341.4 1.5 fusion.17
  342.9 1.5 fusion.29
  347.0 20.8 %reduce-scatter.5.cloned.1.call-done = bf16[768,32]{0,1:T(8,128)(2,1)} async-done(((bf16[3072,32]{0,1:T(8,128)(2,1)}), bf16[768,32]{0,1:T(8,128)(2,1)}) %reduce-scatter.5.cloned.1.call-update) | async-done | bytes 49168 | tf_op jit(solution)/shard_map/reduce_scatter | solution.py:176
  367.8 1.5 fusion.77
  (222 shorter events, 46.1 us)
Async XLA Ops:
  7.2 199.4 %copy-start = (bf16[1,384,3072]{2,1,0:T(8,128)(2,1)S(1)}, bf16[1,384,3072]{2,1,0:T(8,128)(2,1)}, u32[]{:S(2)}) copy-start(bf16[1,384,3072]{2,1,0:T(8,128)(2,1)} %param.12) | copy-start | bytes 7077892
  7.2 129.5 %all-gather.6.cloned.1.call-start = ((), (), s32[]{:S(2)}) async-start(), calls=%async_computation.2 | async-start | bytes 1622016 | tf_op jit(solution)/shard_map/all_gather | solution.py:149
  7.3 241.3 %copy-start.28 = (pred[32]{0:T(512)(128)(4,1)}, pred[32]{0:T(512)(128)(4,1)S(1)}, u32[]{:S(2)}) copy-start(pred[32]{0:T(512)(128)(4,1)S(1)} %fusion.119) | copy-start | bytes 100
  82.1 2.9 copy-start.34
  83.1 4.7 %copy-start.36 = (s32[4]{0:T(128)S(1)}, s32[4]{0:T(128)}, u32[]{:S(2)}) copy-start(s32[4]{0:T(128)} %param.15) | copy-start | bytes 52
  83.8 55.3 %copy-start.31 = (f32[64]{0:T(128)}, f32[64]{0:T(128)S(1)}, u32[]{:S(2)}) copy-start(f32[64]{0:T(128)S(1)} %get-tuple-element.47) | copy-start | bytes 772
  83.9 4.3 %copy-start.30 = (f32[384]{0:T(512)}, f32[384]{0:T(512)S(1)}, u32[]{:S(2)}) copy-start(f32[384]{0:T(512)S(1)} %mul.449) | copy-start | bytes 4612
  84.0 4.2 %copy-start.23 = (f32[384]{0:T(512)}, f32[384]{0:T(512)S(1)}, u32[]{:S(2)}) copy-start(f32[384]{0:T(512)S(1)} %mul.459) | copy-start | bytes 4612
  84.4 54.8 %copy-start.33 = (pred[384]{0:T(512)(128)(4,1)}, pred[384]{0:T(512)(128)(4,1)S(1)}, u32[]{:S(2)}) copy-start(pred[384]{0:T(512)(128)(4,1)S(1)} %fusion.111) | copy-start | bytes 1156
  85.3 3.1 copy-start.8
  85.4 3.1 copy-start.9
  85.5 3.0 copy-start.6
  85.6 2.9 copy-start.7
  86.4 103.3 %all-gather.10.cloned.1.call-start = ((), (), s32[]{:S(2)}) async-start(), calls=%async_computation.6 | async-start | bytes 1622016 | tf_op jit(solution)/shard_map/all_gather | solution.py:150
  87.1 142.1 %reduce-scatter.3.cloned.1.call-start = ((), (), s32[]{:S(2)}) async-start(), calls=%async_computation.3 | async-start | bytes 245760 | tf_op jit(solution)/shard_map/reduce_scatter | solution.py:176
  88.3 116.4 %copy-start.2 = (pred[32,1024]{1,0:T(8,128)(4,1)}, pred[32,1024]{1,0:T(8,128)(4,1)S(1)}, u32[]{:S(2)}) copy-start(pred[32,1024]{1,0:T(8,128)(4,1)S(1)} %broadcast_compare_fusion) | copy-start | bytes 98308
  204.7 24.6 %copy-start.16 = (bf16[32,768]{1,0:T(8,128)(2,1)S(1)}, bf16[32,768]{1,0:T(8,128)(2,1)}, u32[]{:S(2)}) copy-start(bf16[32,768]{1,0:T(8,128)(2,1)} %param.9) | copy-start | bytes 147460
  207.8 123.7 %all-gather.8.cloned.1.call-start = ((), (), s32[]{:S(2)}) async-start(), calls=%async_computation.4 | async-start | bytes 1622016 | tf_op jit(solution)/shard_map/all_gather | solution.py:149
  208.0 40.5 %copy-start.24 = (f32[768]{0:T(1024)}, f32[768]{0:T(1024)S(1)}, u32[]{:S(2)}) copy-start(f32[768]{0:T(1024)S(1)} %get-tuple-element.2) | copy-start | bytes 9220
  208.0 40.5 %copy-start.26 = (f32[768]{0:T(1024)}, f32[768]{0:T(1024)S(1)}, u32[]{:S(2)}) copy-start(f32[768]{0:T(1024)S(1)} %get-tuple-element.3) | copy-start | bytes 9220
  230.2 18.4 %copy-start.14 = (bf16[32,768]{1,0:T(8,128)(2,1)}, bf16[32,768]{1,0:T(8,128)(2,1)S(1)}, u32[]{:S(2)}) copy-start(bf16[32,768]{1,0:T(8,128)(2,1)S(1)} %fusion.65) | copy-start | bytes 147460
  230.2 5.2 %collective-permute-start = (bf16[32,768]{1,0:T(8,128)(2,1)S(1)}, bf16[32,768]{1,0:T(8,128)(2,1)S(1)}, u32[]{:S(2)}, u32[]{:S(2)}) collective-permute-start(bf16[32,768]{1,0:T(8,128)(2,1)S(1)} %fusion.65), channel_id=1, source_target_pairs={{0,128},{1,129},{2,130},{3,131},{4,132},{5,133},{6,134},{7,135},{8... | collective-permute-start | bytes 147464 | tf_op jit(solution)/shard_map/ppermute | solution.py:15
  279.6 88.2 %reduce-scatter.5.cloned.1.call-start = ((), (), s32[]{:S(2)}) async-start(), calls=%async_computation.5 | async-start | bytes 245760 | tf_op jit(solution)/shard_map/reduce_scatter | solution.py:176
  285.6 50.9 %copy-start.5 = (bf16[32,6,64]{2,0,1:T(8,128)(2,1)S(1)}, bf16[32,6,64]{2,0,1:T(8,128)(2,1)}, u32[]{:S(2)}) copy-start(bf16[32,6,64]{2,0,1:T(8,128)(2,1)} %fusion.71) | copy-start | bytes 73732
  334.2 3.7 copy-start.3
  339.0 3.8 %copy-start.1 = (f32[6,32,1024]{2,1,0:T(8,128)S(1)}, f32[6,32,1024]{2,1,0:T(8,128)}, u32[]{:S(2)}) copy-start(f32[6,32,1024]{2,1,0:T(8,128)} %get-tuple-element.54) | copy-start | bytes 2359300
  341.4 3.0 copy-start.4
  344.5 23.3 %copy-start.15 = (bf16[32,768]{1,0:T(8,128)(2,1)S(1)}, bf16[32,768]{1,0:T(8,128)(2,1)}, u32[]{:S(2)}) copy-start(bf16[32,768]{1,0:T(8,128)(2,1)} %copy-done.14) | copy-start | bytes 147460
  344.5 23.3 %copy-start.18 = (bf16[32,768]{1,0:T(8,128)(2,1)S(1)}, bf16[32,768]{1,0:T(8,128)(2,1)}, u32[]{:S(2)}) copy-start(bf16[32,768]{1,0:T(8,128)(2,1)} %copy-done.17) | copy-start | bytes 147460
  344.5 23.3 %copy-start.25 = (f32[768]{0:T(1024)S(1)}, f32[768]{0:T(1024)}, u32[]{:S(2)}) copy-start(f32[768]{0:T(1024)} %copy-done.24) | copy-start | bytes 9220
  344.5 23.3 %copy-start.27 = (f32[768]{0:T(1024)S(1)}, f32[768]{0:T(1024)}, u32[]{:S(2)}) copy-start(f32[768]{0:T(1024)} %copy-done.26) | copy-start | bytes 9220
  344.5 23.3 %copy-start.29 = (pred[32]{0:T(512)(128)(4,1)S(1)}, pred[32]{0:T(512)(128)(4,1)}, u32[]{:S(2)}) copy-start(pred[32]{0:T(512)(128)(4,1)} %copy-done.28) | copy-start | bytes 100
  (11 other events, 14.1 us)
Sparse Core Ops, SparseCore 0:
  86.5 50.1 all-gather.5
  139.3 50.2 all-gather.9
  208.0 21.2 reduce-scatter.2
  279.7 51.7 all-gather.7
  346.4 21.3 reduce-scatter.4
where the time goes:
time: 378 us; the launch traced here: 376 us
  waiting for transfers between devices  188 us (50%)
  blocking collectives  77.7 us (21%)
  local copies, waits for them, and re-layouts  47.8 us (13%)
  matrix products  23.4 us (6%)
  other arithmetic  19 us (5%)
  between operations  16.1 us (4%)
  starting transfers between devices  3.86 us (1%)
    all_gather x2, waiting for transfers between devices, attend(): lax.all_gather(fresh_kv, 'seq', axis=1, tiled=True)  94.1 us
    all_gather x1, waiting for transfers between devices, attend(): lax.all_gather(stale_own, 'seq', axis=1, tiled=True)  49.3 us
    all_gather x1, blocking collectives, local(): lax.all_gather(jnp.pad(by_tp.reshape(1, 4, -1), ((0, 0), (0, 4), (0, 0)))...  42.5 us
    reduce_scatter x2, waiting for transfers between devices, run_layer(): lax.psum_scatter(lax.dot_general(weights_out, attended, (((0,), (1,)), ((...  42 us
    all_gather x2, blocking collectives, run_layer(): lax.all_gather(incoming, 'tp', axis=1, tiled=True).astype(jnp.float32)  24.5 us
    unnamed x1, blocking collectives  10.7 us
    dot_general x2, matrix products, run_layer(): jnp.einsum('td,dcf->tcf', normed, weights_qkv, preferred_element_type=jnp...  8.79 us
    slice x4, local copies, waits for them, and re-layouts, merge_block(): fresh_keys = fresh_block[0].reshape(key_count, head_count, HEAD)  8.52 us
  transfers between devices with their start and end apart: 6, of which 6 were waited for; matrix products, arithmetic and copies ran while one was open for 3% of the time, Pallas kernels for 0%

commit v1 on v0

--- a/solution.py
+++ b/solution.py
@@ -1,3 +1,4 @@
+import functools
 import math
 import jax
 import jax.numpy as jnp
@@ -7,6 +8,27 @@
 HEAD = 64
 TEMB = 512
 TEXT = 226
+
+
+def draft_sample(chunk, along_axis):
+    n_blocks = lax.axis_size(along_axis)
+    leaves = [(k0, (k0 + 1) % n_blocks) for k0 in range(n_blocks)]
+    x_next, y2 = ([chunk], [chunk])
+    inbox = [(k0, (k0 - 1) % n_blocks) for k0 in range(n_blocks)]
+    for _ in range(n_blocks // 2):
+        reached = lax.ppermute(x_next[-1], along_axis, leaves)
+        x_next.append(reached)
+    for _ in [*range((n_blocks - 1) // 2)]:
+        low = lax.ppermute(y2[-1], along_axis, inbox)
+        y2.append(low)
+    m_next = jnp.concatenate([*x_next[::-1], *y2[1:]], axis=1)
+    value_now = jnp.roll(
+        m_next, shift=(lax.axis_index(along_axis) - n_blocks // 2) * chunk.shape[1], axis=1
+    )
+    return value_now
+
+
+cut_roots_on_mesh = functools.partial(draft_sample, along_axis="tp")
 
 
 def shifted(value, axis, steps):
@@ -154,7 +176,7 @@
         return jnp.transpose(blended, (1, 0, 2)).reshape(tok_rows, head_cols).astype(jnp.bfloat16)
 
     def run_layer(incoming):
-        features_all = lax.all_gather(incoming, "tp", axis=1, tiled=True).astype(jnp.float32)
+        features_all = cut_roots_on_mesh(incoming).astype(jnp.float32)
         average = jnp.mean(features_all, axis=1, keepdims=True)
         centred = features_all - average
         variance = jnp.mean(centred * centred, axis=1, keepdims=True)

time: 378 us -> 316 us (0.84)
  waiting for transfers between devices: 188 us -> 142 us
  blocking collectives: 77.7 us -> 52.2 us
  starting transfers between devices: 3.86 us -> 11.3 us
    all_gather x1, waiting for transfers between devices: 49.3 us -> 0.02 us  [attend(): lax.all_gather(stale_own, 'seq', axis=1, tiled=True)]
    all_gather x2 -> x0, blocking collectives: 24.5 us -> none  [run_layer(): lax.all_gather(incoming, 'tp', axis=1, tiled=True).astype(jnp.float32)]
    ppermute x0 -> x6, waiting for transfers between devices: none -> 11.5 us  [the longest x4 11.5 us: draft_sample(): reached = lax.ppermute(x_next[-1], along_axis, leaves)]
    ppermute x0 -> x6, starting transfers between devices: none -> 7.65 us  [the longest x2 4.89 us: draft_sample(): low = lax.ppermute(y2[-1], along_axis, inbox)]
    all_gather x2, waiting for transfers between devices: 94.1 us -> 86.5 us  [attend(): lax.all_gather(fresh_kv, 'seq', axis=1, tiled=True)]
  transfers between devices with their start and end apart: 6 -> 12, of which waited for: 6 -> 8; matrix products, arithmetic and copies ran while one was open for 3% -> 9% of each run, Pallas kernels for 0% -> 0%
where the time goes in v1:
time: 316 us; the launch traced here: 314 us
  waiting for transfers between devices  142 us (45%)
  blocking collectives  52.2 us (17%)
  local copies, waits for them, and re-layouts  49.4 us (16%)
  other arithmetic  21.9 us (7%)
  matrix products  21.4 us (7%)
  between operations  16 us (5%)
  starting transfers between devices  11.3 us (4%)
    all_gather x2, waiting for transfers between devices, attend(): lax.all_gather(fresh_kv, 'seq', axis=1, tiled=True)  86.5 us
    all_gather x1, blocking collectives, local(): lax.all_gather(jnp.pad(by_tp.reshape(1, 4, -1), ((0, 0), (0, 4), (0, 0)))...  42.6 us
    reduce_scatter x2, waiting for transfers between devices, run_layer(): lax.psum_scatter(lax.dot_general(weights_out, attended, (((0,), (1,)), ((...  42 us
    ppermute x4, waiting for transfers between devices, draft_sample(): reached = lax.ppermute(x_next[-1], along_axis, leaves)  11.5 us
    slice x4, local copies, waits for them, and re-layouts, merge_block(): fresh_keys = fresh_block[0].reshape(key_count, head_count, HEAD)  9.97 us
    unnamed x1, blocking collectives  9.51 us
    dot_general x2, matrix products, run_layer(): jnp.einsum('td,dcf->tcf', normed, weights_qkv, preferred_element_type=jnp...  8.79 us
    sub x10, local copies, waits for them, and re-layouts, head_norm(): centred = parts - average  7.57 us
  transfers between devices with their start and end apart: 12, of which 8 were waited for; matrix products, arithmetic and copies ran while one was open for 9% of the time, Pallas kernels for 0%

profile of v1, /device:TPU:2, one launch (start us, length us, event | category | flops | bytes accessed | tf_op | source)
XLA Modules:
  0.0 314.1 jit_solution(4986793873058801983)
XLA Ops:
  7.2 1.7 collective-permute-start
  8.9 1.7 collective-permute-start.2
  14.5 9.5 %all-reduce.1 = f32[576]{0:T(1024)S(1)} all-reduce(f32[576]{0:T(1024)S(1)} %dynamic-update-slice), channel_id=2, replica_groups=mesh['section'=2,'seq'=32,'tp'=4] {'tp'}, use_global_device_ids=true, to_apply=%add.1 | all-reduce | flops 576 | bytes 4608
  24.1 42.6 %all_gather.17 = f32[32,8,144]{2,1,0:T(8,128)S(1)} all-gather(f32[1,8,144]{2,1,0:T(8,128)S(1)} %pad.4), channel_id=1, replica_groups=mesh['section'=2,'seq'=32,'tp'=4] {'seq'}, dimensions={0}, use_global_device_ids=true | all-gather | bytes 152064 | tf_op jit(solution)/shard_map/all_gather | solution.py:143
  70.4 3.7 %collective-permute-done.1 = bf16[32,768]{1,0:T(8,128)(2,1)S(1)} collective-permute-done((bf16[32,768]{1,0:T(8,128)(2,1)S(1)}, bf16[32,768]{1,0:T(8,128)(2,1)S(1)}, u32[]{:S(2)}, u32[]{:S(2)}) %collective-permute-start.1) | collective-permute-done | bytes 49184 | tf_op jit(solution)/shard_map/ppermute | solution.py:19
  75.9 4.4 %fusion.2 = f32[32,3,384]{2,0,1:T(8,128)S(1)} fusion(bf16[1,3072,3,384]{3,1,2,0:T(8,128)(2,1)} %param.12, bf16[32,3072]{1,0:T(8,128)(2,1)S(1)} %get-tuple-element.8, f32[3072]{0:T(1024)S(1)} %bitcast.178, f32[3072]{0:T(1024)S(1)} %bitcast.180, f32[3072]{0:T(1024)S(1)} %bitcast.182, f32[3072]{0:T(1024)S(1)} %bitcast.176, f32[32]{0:T(128)S(1)} %add_rsqrt_fusion.5, ...), kind=kOutput, calls=%fused_computation.2 | convolution fusion | flops 227377152 | bytes 7471392 | tf_op jit(solution)/shard_map/td,dcf->tcf/dot_general | solution.py:186
  85.2 2.7 fusion.143
  89.3 2.3 copy.168
  91.6 41.6 %all-gather.6.cloned.1.call-done = bf16[2,1024,384]{2,1,0:T(8,128)(2,1)} async-done(((bf16[2,32,384]{2,1,0:T(8,128)(2,1)}), bf16[2,1024,384]{2,1,0:T(8,128)(2,1)}) %all-gather.6.cloned.1.call-update) | async-done | bytes 1572880 | tf_op jit(solution)/shard_map/all_gather | solution.py:171
  133.2 2.7 fusion.144
  135.9 2.3 copy.165
  140.7 2.3 copy.167
  143.0 1.5 fusion.16
  144.5 1.8 fusion.28
  148.3 21.3 %reduce-scatter.3.cloned.1.call-done = bf16[768,32]{0,1:T(8,128)(2,1)} async-done(((bf16[3072,32]{0,1:T(8,128)(2,1)}), bf16[768,32]{0,1:T(8,128)(2,1)}) %reduce-scatter.3.cloned.1.call-update) | async-done | bytes 49168 | tf_op jit(solution)/shard_map/reduce_scatter | solution.py:198
  170.5 3.5 %collective-permute-start.3 = (bf16[32,768]{1,0:T(8,128)(2,1)S(1)}, bf16[32,768]{1,0:T(8,128)(2,1)S(1)}, u32[]{:S(2)}, u32[]{:S(2)}) collective-permute-start(bf16[32,768]{1,0:T(8,128)(2,1)S(1)} %fusion.79), channel_id=1, source_target_pairs={{0,128},{1,129},{2,130},{3,131},{4,132},{5,133},{6,134},{7,135},{8... | collective-permute-start | bytes 147464 | tf_op jit(solution)/shard_map/ppermute | solution.py:37
  174.0 1.7 collective-permute-done.3
  175.7 3.2 %collective-permute-start.6 = (bf16[32,768]{1,0:T(8,128)(2,1)S(1)}, bf16[32,768]{1,0:T(8,128)(2,1)S(1)}, u32[]{:S(2)}, u32[]{:S(2)}) collective-permute-start(bf16[32,768]{1,0:T(8,128)(2,1)S(1)} %collective-permute-done.3), channel_id=1, source_target_pairs={{0,3},{1,0},{2,1},{3,2},{4,7},{5,4},{6,5},{7,6},{8,11},{9,8},{10,9... | collective-permute-start | bytes 147464 | tf_op jit(solution)/shard_map/ppermute | solution.py:22
  179.0 2.5 collective-permute-done.4
  181.5 5.3 %collective-permute-done.5 = bf16[32,768]{1,0:T(8,128)(2,1)S(1)} collective-permute-done((bf16[32,768]{1,0:T(8,128)(2,1)S(1)}, bf16[32,768]{1,0:T(8,128)(2,1)S(1)}, u32[]{:S(2)}, u32[]{:S(2)}) %collective-permute-start.5) | collective-permute-done | bytes 49184 | tf_op jit(solution)/shard_map/ppermute | solution.py:19
  187.9 4.4 %fusion = f32[32,3,384]{2,0,1:T(8,128)S(1)} fusion(bf16[1,3072,3,384]{3,1,2,0:T(8,128)(2,1)} %param.12, bf16[32,3072]{1,0:T(8,128)(2,1)S(1)} %get-tuple-element.6, f32[32]{0:T(128)S(1)} %add_rsqrt_fusion.4, f32[32]{0:T(128)S(1)} %broadcast_multiply_fusion.7, f32[3072]{0:T(1024)S(1)} %bitcast.179, f32[3072]{0:T(1024)S(1)} %bitcast.181, f32[3072]{0:T(1024)S(1)} %bitcast.183, ...), kind=kOutput, calls=%fused_computation | convolution fusion | flops 227377152 | bytes 7471392 | tf_op jit(solution)/shard_map/td,dcf->tcf/dot_general | solution.py:186
  203.7 1.6 mul.484
  206.8 1.6 sub.171
  209.9 1.6 sub.177
  211.5 1.5 fusion.107
  224.8 44.9 %all-gather.8.cloned.1.call-done = bf16[2,1024,384]{2,1,0:T(8,128)(2,1)} async-done(((bf16[2,32,384]{2,1,0:T(8,128)(2,1)}), bf16[2,1024,384]{2,1,0:T(8,128)(2,1)}) %all-gather.8.cloned.1.call-update) | async-done | bytes 1572880 | tf_op jit(solution)/shard_map/all_gather | solution.py:171
  269.7 2.7 fusion.142
  272.4 2.3 copy.180
  277.3 2.4 copy.181
  281.1 1.5 fusion.29
  285.2 20.8 %reduce-scatter.5.cloned.1.call-done = bf16[768,32]{0,1:T(8,128)(2,1)} async-done(((bf16[3072,32]{0,1:T(8,128)(2,1)}), bf16[768,32]{0,1:T(8,128)(2,1)}) %reduce-scatter.5.cloned.1.call-update) | async-done | bytes 49168 | tf_op jit(solution)/shard_map/reduce_scatter | solution.py:198
  306.0 1.5 fusion.91
  (232 shorter events, 53.1 us)
Async XLA Ops:
  7.2 139.7 %copy-start = (bf16[1,384,3072]{2,1,0:T(8,128)(2,1)S(1)}, bf16[1,384,3072]{2,1,0:T(8,128)(2,1)}, u32[]{:S(2)}) copy-start(bf16[1,384,3072]{2,1,0:T(8,128)(2,1)} %param.14) | copy-start | bytes 7077892
  7.2 78.0 %all-gather.10.cloned.1.call-start = ((), (), s32[]{:S(2)}) async-start(), calls=%async_computation.6 | async-start | bytes 1622016 | tf_op jit(solution)/shard_map/all_gather | solution.py:172
  7.2 61.5 %collective-permute-start = (bf16[32,768]{1,0:T(8,128)(2,1)}, bf16[32,768]{1,0:T(8,128)(2,1)S(1)}, u32[]{:S(2)}, u32[]{:S(2)}) collective-permute-start(bf16[32,768]{1,0:T(8,128)(2,1)} %param.11), channel_id=1, source_target_pairs={{0,1},{1,2},{2,3},{3,0},{4,5},{5,6},{6,7},{7,4},{8,9},{9,10},{10,1... | collective-permute-start | bytes 147464 | tf_op jit(solution)/shard_map/ppermute | solution.py:19
  8.9 61.5 %collective-permute-start.2 = (bf16[32,768]{1,0:T(8,128)(2,1)}, bf16[32,768]{1,0:T(8,128)(2,1)S(1)}, u32[]{:S(2)}, u32[]{:S(2)}) collective-permute-start(bf16[32,768]{1,0:T(8,128)(2,1)} %param.11), channel_id=1, source_target_pairs={{0,3},{1,0},{2,1},{3,2},{4,7},{5,4},{6,5},{7,6},{8,11},{9,8},{10,9... | collective-permute-start | bytes 147464 | tf_op jit(solution)/shard_map/ppermute | solution.py:22
  10.6 122.6 %all-gather.6.cloned.1.call-start = ((), (), s32[]{:S(2)}) async-start(), calls=%async_computation.2 | async-start | bytes 1622016 | tf_op jit(solution)/shard_map/all_gather | solution.py:171
  67.8 17.2 %copy-start.33 = (f32[64]{0:T(128)}, f32[64]{0:T(128)S(1)}, u32[]{:S(2)}) copy-start(f32[64]{0:T(128)S(1)} %get-tuple-element.52) | copy-start | bytes 772
  68.7 14.3 %copy-start.35 = (pred[384]{0:T(512)(128)(4,1)}, pred[384]{0:T(512)(128)(4,1)S(1)}, u32[]{:S(2)}) copy-start(pred[384]{0:T(512)(128)(4,1)S(1)} %fusion.125) | copy-start | bytes 1156
  68.8 5.4 %collective-permute-start.1 = (bf16[32,768]{1,0:T(8,128)(2,1)S(1)}, bf16[32,768]{1,0:T(8,128)(2,1)S(1)}, u32[]{:S(2)}, u32[]{:S(2)}) collective-permute-start(bf16[32,768]{1,0:T(8,128)(2,1)S(1)} %collective-permute-done), channel_id=1, source_target_pairs={{0,1},{1,2},{2,3},{3,0},{4,5},{5,6},{6,7},{7,4},{8,9},{9,10},{10,1... | collective-permute-start | bytes 147464 | tf_op jit(solution)/shard_map/ppermute | solution.py:19
  69.9 118.0 %copy-start.30 = (pred[32]{0:T(512)(128)(4,1)}, pred[32]{0:T(512)(128)(4,1)S(1)}, u32[]{:S(2)}) copy-start(pred[32]{0:T(512)(128)(4,1)S(1)} %fusion.133) | copy-start | bytes 100
  70.0 13.0 %copy-start.25 = (f32[384]{0:T(512)}, f32[384]{0:T(512)S(1)}, u32[]{:S(2)}) copy-start(f32[384]{0:T(512)S(1)} %mul.464) | copy-start | bytes 4612
  70.1 14.9 %copy-start.10 = (f32[32,64]{1,0:T(8,128)}, f32[32,64]{1,0:T(8,128)S(1)}, u32[]{:S(2)}) copy-start(f32[32,64]{1,0:T(8,128)S(1)} %copy.155) | copy-start | bytes 24580
  70.2 14.8 %copy-start.11 = (f32[32,64]{1,0:T(8,128)}, f32[32,64]{1,0:T(8,128)S(1)}, u32[]{:S(2)}) copy-start(f32[32,64]{1,0:T(8,128)S(1)} %copy.160) | copy-start | bytes 24580
  70.3 12.7 %copy-start.8 = (f32[1,32,384]{2,1,0:T(8,128)}, f32[1,32,384]{2,1,0:T(8,128)S(1)}, u32[]{:S(2)}) copy-start(f32[1,32,384]{2,1,0:T(8,128)S(1)} %tile.20) | copy-start | bytes 147460
  70.4 12.6 %copy-start.9 = (f32[1,32,384]{2,1,0:T(8,128)}, f32[1,32,384]{2,1,0:T(8,128)S(1)}, u32[]{:S(2)}) copy-start(f32[1,32,384]{2,1,0:T(8,128)S(1)} %tile.21) | copy-start | bytes 147460
  83.8 85.8 %reduce-scatter.3.cloned.1.call-start = ((), (), s32[]{:S(2)}) async-start(), calls=%async_computation.3 | async-start | bytes 245760 | tf_op jit(solution)/shard_map/reduce_scatter | solution.py:198
  84.4 61.9 %copy-start.3 = (pred[32,1024]{1,0:T(8,128)(4,1)}, pred[32,1024]{1,0:T(8,128)(4,1)S(1)}, u32[]{:S(2)}) copy-start(pred[32,1024]{1,0:T(8,128)(4,1)S(1)} %broadcast_compare_fusion) | copy-start | bytes 98308
  146.3 23.3 %copy-start.16 = (bf16[32,768]{1,0:T(8,128)(2,1)S(1)}, bf16[32,768]{1,0:T(8,128)(2,1)}, u32[]{:S(2)}) copy-start(bf16[32,768]{1,0:T(8,128)(2,1)} %param.11) | copy-start | bytes 147460
  148.1 121.6 %all-gather.8.cloned.1.call-start = ((), (), s32[]{:S(2)}) async-start(), calls=%async_computation.4 | async-start | bytes 1622016 | tf_op jit(solution)/shard_map/all_gather | solution.py:171
  148.3 25.7 %copy-start.26 = (f32[768]{0:T(1024)}, f32[768]{0:T(1024)S(1)}, u32[]{:S(2)}) copy-start(f32[768]{0:T(1024)S(1)} %get-tuple-element.3) | copy-start | bytes 9220
  148.3 25.7 %copy-start.28 = (f32[768]{0:T(1024)}, f32[768]{0:T(1024)S(1)}, u32[]{:S(2)}) copy-start(f32[768]{0:T(1024)S(1)} %get-tuple-element.4) | copy-start | bytes 9220
  170.5 21.8 %copy-start.17 = (bf16[32,768]{1,0:T(8,128)(2,1)}, bf16[32,768]{1,0:T(8,128)(2,1)S(1)}, u32[]{:S(2)}) copy-start(bf16[32,768]{1,0:T(8,128)(2,1)S(1)} %fusion.79) | copy-start | bytes 147460
  170.5 5.2 %collective-permute-start.3 = (bf16[32,768]{1,0:T(8,128)(2,1)S(1)}, bf16[32,768]{1,0:T(8,128)(2,1)S(1)}, u32[]{:S(2)}, u32[]{:S(2)}) collective-permute-start(bf16[32,768]{1,0:T(8,128)(2,1)S(1)} %fusion.79), channel_id=1, source_target_pairs={{0,128},{1,129},{2,130},{3,131},{4,132},{5,133},{6,134},{7,135},{8... | collective-permute-start | bytes 147464 | tf_op jit(solution)/shard_map/ppermute | solution.py:37
  175.7 5.7 %collective-permute-start.4 = (bf16[32,768]{1,0:T(8,128)(2,1)S(1)}, bf16[32,768]{1,0:T(8,128)(2,1)S(1)}, u32[]{:S(2)}, u32[]{:S(2)}) collective-permute-start(bf16[32,768]{1,0:T(8,128)(2,1)S(1)} %collective-permute-done.3), channel_id=1, source_target_pairs={{0,1},{1,2},{2,3},{3,0},{4,5},{5,6},{6,7},{7,4},{8,9},{9,10},{10,1... | collective-permute-start | bytes 147464 | tf_op jit(solution)/shard_map/ppermute | solution.py:19
  175.7 5.7 %collective-permute-start.6 = (bf16[32,768]{1,0:T(8,128)(2,1)S(1)}, bf16[32,768]{1,0:T(8,128)(2,1)S(1)}, u32[]{:S(2)}, u32[]{:S(2)}) collective-permute-start(bf16[32,768]{1,0:T(8,128)(2,1)S(1)} %collective-permute-done.3), channel_id=1, source_target_pairs={{0,3},{1,0},{2,1},{3,2},{4,7},{5,4},{6,5},{7,6},{8,11},{9,8},{10,9... | collective-permute-start | bytes 147464 | tf_op jit(solution)/shard_map/ppermute | solution.py:22
  181.5 5.3 %collective-permute-start.5 = (bf16[32,768]{1,0:T(8,128)(2,1)S(1)}, bf16[32,768]{1,0:T(8,128)(2,1)S(1)}, u32[]{:S(2)}, u32[]{:S(2)}) collective-permute-start(bf16[32,768]{1,0:T(8,128)(2,1)S(1)} %collective-permute-done.4), channel_id=1, source_target_pairs={{0,1},{1,2},{2,3},{3,0},{4,5},{5,6},{6,7},{7,4},{8,9},{9,10},{10,1... | collective-permute-start | bytes 147464 | tf_op jit(solution)/shard_map/ppermute | solution.py:19
  218.9 87.1 %reduce-scatter.5.cloned.1.call-start = ((), (), s32[]{:S(2)}) async-start(), calls=%async_computation.5 | async-start | bytes 245760 | tf_op jit(solution)/shard_map/reduce_scatter | solution.py:198
  224.8 49.9 %copy-start.7 = (bf16[32,6,64]{2,0,1:T(8,128)(2,1)S(1)}, bf16[32,6,64]{2,0,1:T(8,128)(2,1)}, u32[]{:S(2)}) copy-start(bf16[32,6,64]{2,0,1:T(8,128)(2,1)} %fusion.85) | copy-start | bytes 73732
  282.7 23.3 %copy-start.18 = (bf16[32,768]{1,0:T(8,128)(2,1)S(1)}, bf16[32,768]{1,0:T(8,128)(2,1)}, u32[]{:S(2)}) copy-start(bf16[32,768]{1,0:T(8,128)(2,1)} %copy-done.17) | copy-start | bytes 147460
  282.7 23.3 %copy-start.20 = (bf16[32,768]{1,0:T(8,128)(2,1)S(1)}, bf16[32,768]{1,0:T(8,128)(2,1)}, u32[]{:S(2)}) copy-start(bf16[32,768]{1,0:T(8,128)(2,1)} %copy-done.19) | copy-start | bytes 147460
  282.7 23.3 %copy-start.27 = (f32[768]{0:T(1024)S(1)}, f32[768]{0:T(1024)}, u32[]{:S(2)}) copy-start(f32[768]{0:T(1024)} %copy-done.26) | copy-start | bytes 9220
  282.8 23.3 %copy-start.29 = (f32[768]{0:T(1024)S(1)}, f32[768]{0:T(1024)}, u32[]{:S(2)}) copy-start(f32[768]{0:T(1024)} %copy-done.28) | copy-start | bytes 9220
  282.8 23.2 %copy-start.31 = (pred[32]{0:T(512)(128)(4,1)S(1)}, pred[32]{0:T(512)(128)(4,1)}, u32[]{:S(2)}) copy-start(pred[32]{0:T(512)(128)(4,1)} %copy-done.30) | copy-start | bytes 100
  (17 other events, 61.3 us)
Sparse Core Ops, SparseCore 0:
  10.7 54.9 all-gather.9
  83.9 49.1 all-gather.5
  148.3 21.2 reduce-scatter.2
  219.1 50.6 all-gather.7
  284.7 21.2 reduce-scatter.4
